TPU v7x, 32 devices: a whole 2x2x4 slice. The times are simulated.
32 devices in a mesh: blk: 4 (over x, core), ulysses: 8 (over z, y).
Axes of the slice: x: 2, y: 2, z: 4, core: 2. Of those that a mesh axis runs over, the one named last changes fastest.
Arguments:
- query_rows: bfloat16 [32, 4096, 128], P(None, ('blk', 'ulysses')), may hold values from -160 to 160
- out_grad: bfloat16 [32, 4096, 128], P(None, ('blk', 'ulysses')), may hold values from -6 to 6
- key_rows: bfloat16 [32, 512, 128], P(None, 'blk'), may hold values from -6 to 6
- value_rows: bfloat16 [32, 512, 128], P(None, 'blk'), may hold values from -6 to 6
- routes: int32 [4, 4], replicated, may hold values from 0 to 7
Outputs:
- query_grad: bfloat16 [32, 4096, 128], P(None, ('blk', 'ulysses'))
- key_grad: float32 [32, 512, 128], P(None, ('blk', 'ulysses'))
- value_grad: float32 [32, 512, 128], P(None, ('blk', 'ulysses'))
All inputs are finite; a program needn't handle non-finite values.
Results may differ from a plain program's by a relative error of at most 0.0056.
Values may be sent and summed in bfloat16 or wider, within the bound.
No kernel may reach another device: no remote copies, remote signals or barrier semaphores. Data moves between devices by JAX's collectives and lax.ppermute only.
A program may use at most 64 MiB of HBM per device.

v0:
```python
import math
import jax
import jax.numpy as jnp
from jax import lax
from jax.sharding import PartitionSpec as P

KB = 16


def body(query_rows, out_grad, key_rows, value_rows, routes):
    head_count, token_count, head_dim = query_rows.shape
    group_keys = key_rows.shape[1]
    cycle_size = lax.axis_size("blk")
    group_size = lax.axis_size("ulysses")
    sub_count = max(1, group_size // head_count)
    item_count = head_count * sub_count // group_size
    sub_length = token_count // sub_count
    row_count = group_size * sub_length
    block_count = group_keys // KB
    key_stride = token_count * group_size // group_keys
    score_scale = 1.0 / math.sqrt(head_dim)
    my_group = lax.axis_index("blk")
    my_rank = lax.axis_index("ulysses")
    packed_query = query_rows.reshape(head_count * sub_count, sub_length, head_dim)
    packed_grad = out_grad.reshape(head_count * sub_count, sub_length, head_dim)
    local_query, local_grad = (
        lax.all_to_all(packed_query, "ulysses", split_axis=0, concat_axis=1, tiled=True),
        lax.all_to_all(packed_grad, "ulysses", split_axis=0, concat_axis=1, tiled=True),
    )
    first_head = my_rank * item_count // sub_count
    own_keys = lax.dynamic_slice_in_dim(key_rows, first_head, item_count, 0)
    own_values = lax.dynamic_slice_in_dim(value_rows, first_head, item_count, 0)
    requested = lax.dynamic_index_in_dim(routes, my_group, 1, keepdims=False)
    block_ids = jnp.arange(block_count, dtype=jnp.int32)
    block_keys = own_keys.reshape(item_count, block_count, KB, head_dim)
    block_values = own_values.reshape(item_count, block_count, KB, head_dim)
    far_keys, far_values = (
        lax.all_to_all(
            jnp.take(block_keys, requested, axis=1), "blk", split_axis=1, concat_axis=1, tiled=True
        ),
        lax.all_to_all(
            jnp.take(block_values, requested, axis=1),
            "blk",
            split_axis=1,
            concat_axis=1,
            tiled=True,
        ),
    )
    near_keys = jnp.concatenate(
        [own_keys, far_keys.reshape(item_count, cycle_size * KB, head_dim)], axis=1
    )
    near_values = jnp.concatenate(
        [own_values, far_values.reshape(item_count, cycle_size * KB, head_dim)], axis=1
    )
    near_count = near_keys.shape[1]
    item_sub = (my_rank * item_count + jnp.arange(item_count, dtype=jnp.int32)) % sub_count
    far_visible = jnp.repeat(jnp.arange(cycle_size, dtype=jnp.int32) < my_group, KB)
    own_offsets = jnp.arange(group_keys, dtype=jnp.int32) * key_stride
    block_rows = 1024

    def attend(row_block, carried):
        query_out, key_acc, value_acc = carried
        row_start = row_block * block_rows
        queries = lax.dynamic_slice_in_dim(local_query, row_start, block_rows, 1)
        grad_rows = lax.dynamic_slice_in_dim(local_grad, row_start, block_rows, 1)
        row_ids = row_start + jnp.arange(block_rows, dtype=jnp.int32)
        positions = (
            row_ids[None, :] // sub_length * token_count
            + item_sub[:, None] * sub_length
            + row_ids[None, :] % sub_length
        )
        own_visible = own_offsets[None, None, :] <= positions[:, :, None]
        visible = jnp.concatenate(
            [
                own_visible,
                jnp.broadcast_to(far_visible, (item_count, block_rows, far_visible.shape[0])),
            ],
            axis=2,
        )
        scores = (
            jnp.einsum("ird,ikd->irk", queries, near_keys, preferred_element_type=jnp.float32)
            * score_scale
        )
        row_max = jnp.max(jnp.where(visible, scores, -jnp.inf), axis=-1, keepdims=True)
        expsum = jnp.where(visible, jnp.exp(scores - row_max), 0.0)
        weights = expsum / jnp.sum(expsum, axis=-1, keepdims=True)
        weights_half = weights.astype(jnp.bfloat16)
        attended = jnp.einsum(
            "irk,ikd->ird", weights_half, near_values, preferred_element_type=jnp.float32
        )
        delta_rows = jnp.sum(grad_rows.astype(jnp.float32) * attended, axis=-1, keepdims=True)
        dweights = jnp.einsum(
            "ird,ikd->irk", grad_rows, near_values, preferred_element_type=jnp.float32
        )
        dscore = (weights * (dweights - delta_rows)).astype(jnp.bfloat16)
        query_part = (
            jnp.einsum("irk,ikd->ird", dscore, near_keys, preferred_element_type=jnp.float32)
            * score_scale
        ).astype(jnp.bfloat16)
        key_acc = (
            key_acc
            + jnp.einsum("irk,ird->ikd", dscore, queries, preferred_element_type=jnp.float32)
            * score_scale
        )
        value_acc = value_acc + jnp.einsum(
            "irk,ird->ikd", weights_half, grad_rows, preferred_element_type=jnp.float32
        )
        query_out = lax.dynamic_update_slice_in_dim(query_out, query_part, row_start, 1)
        return (query_out, key_acc, value_acc)

    start_state = (
        jnp.zeros((item_count, row_count, head_dim), jnp.bfloat16),
        jnp.zeros((item_count, near_count, head_dim), jnp.float32),
        jnp.zeros((item_count, near_count, head_dim), jnp.float32),
    )
    query_out, key_acc, value_acc = lax.fori_loop(0, row_count // block_rows, attend, start_state)
    own_key_grad = key_acc[:, :group_keys]
    own_value_grad = value_acc[:, :group_keys]
    far_key_grad = key_acc[:, group_keys:].reshape(item_count, cycle_size, KB, head_dim)
    far_value_grad = value_acc[:, group_keys:].reshape(item_count, cycle_size, KB, head_dim)
    back_keys, back_values = (
        lax.all_to_all(far_key_grad, "blk", split_axis=1, concat_axis=1, tiled=True),
        lax.all_to_all(far_value_grad, "blk", split_axis=1, concat_axis=1, tiled=True),
    )
    placer = (requested[:, None] == block_ids[None, :]).astype(jnp.float32)
    added_keys = jnp.einsum(
        "gb,igkd->ibkd", placer, back_keys, precision=lax.Precision.HIGHEST
    ).reshape(item_count, group_keys, head_dim)
    added_values = jnp.einsum(
        "gb,igkd->ibkd", placer, back_values, precision=lax.Precision.HIGHEST
    ).reshape(item_count, group_keys, head_dim)
    key_share = (own_key_grad + added_keys).astype(jnp.bfloat16)
    value_share = (own_value_grad + added_values).astype(jnp.bfloat16)
    query_back, key_back, value_back = (
        lax.all_to_all(query_out, "ulysses", split_axis=1, concat_axis=0, tiled=True),
        lax.all_to_all(key_share, "ulysses", split_axis=1, concat_axis=0, tiled=True),
        lax.all_to_all(value_share, "ulysses", split_axis=1, concat_axis=0, tiled=True),
    )
    query_grad = query_back.reshape(head_count, token_count, head_dim)
    key_grad = jnp.sum(
        key_back.astype(jnp.float32).reshape(head_count, sub_count, -1, head_dim), axis=1
    )
    value_grad = jnp.sum(
        value_back.astype(jnp.float32).reshape(head_count, sub_count, -1, head_dim), axis=1
    )
    return (query_grad, key_grad, value_grad)


def solution(mesh):
    return jax.shard_map(
        body,
        mesh=mesh,
        in_specs=(
            P(None, ("blk", "ulysses"), None),
            P(None, ("blk", "ulysses"), None),
            P(None, "blk", None),
            P(None, "blk", None),
            P(),
        ),
        out_specs=(
            P(None, ("blk", "ulysses"), None),
            P(None, ("blk", "ulysses"), None),
            P(None, ("blk", "ulysses"), None),
        ),
        check_vma=False,
    )
```

profile of v0, /device:TPU:0, one launch (start us, length us, event | category | flops | bytes accessed | tf_op | source)
XLA Modules:
  0.0 155.4 jit_solution(3819428733041253633)
XLA Ops:
  1.5 1.0 constant_dynamic-slice_fusion
  3.8 8.2 %all_to_all.92 = bf16[4,4,16,128]{3,2,0,1:T(8,128)(2,1)S(1)} all-to-all(bf16[4,4,16,128]{3,2,0,1:T(8,128)(2,1)S(1)} %get-tuple-element.29), channel_id=1, replica_groups=mesh['blk'=4,'ulysses'=8] {'blk'}, dimensions={1} | all-to-all | bytes 131072 | tf_op jit(solution)/shard_map/all_to_all | solution.py:38
  11.9 6.5 %all_to_all.93 = bf16[4,4,16,128]{3,2,0,1:T(8,128)(2,1)S(1)} all-to-all(bf16[4,4,16,128]{3,2,0,1:T(8,128)(2,1)S(1)} %get-tuple-element.28), channel_id=1, replica_groups=mesh['blk'=4,'ulysses'=8] {'blk'}, dimensions={1} | all-to-all | bytes 131072 | tf_op jit(solution)/shard_map/all_to_all | solution.py:41
  18.4 31.4 %all_to_all.94 = bf16[32,128,128]{2,1,0:T(8,128)(2,1)S(1)} all-to-all(bf16[32,128,128]{2,1,0:T(8,128)(2,1)} %param.7), channel_id=1, replica_groups=mesh['blk'=4,'ulysses'=8] {'ulysses'}, dimensions={0} | all-to-all | bytes 2097152 | tf_op jit(solution)/shard_map/all_to_all | solution.py:27
  49.8 3.6 %all-to-all-start.3 = ((bf16[32,128,128]{2,1,0:T(8,128)(2,1)}), bf16[32,128,128]{2,1,0:T(8,128)(2,1)S(1)}, u32[]{:S(2)}, u32[]{:S(2)}) async-start(bf16[32,128,128]{2,1,0:T(8,128)(2,1)} %param.8), calls=%async_computation.3 | async-start | bytes 2097152 | tf_op jit(solution)/shard_map/all_to_all | solution.py:28
  53.6 1.0 broadcast_compare_fusion
  55.4 23.6 %all-to-all-done.3 = bf16[32,128,128]{2,1,0:T(8,128)(2,1)S(1)} async-done(((bf16[32,128,128]{2,1,0:T(8,128)(2,1)}), bf16[32,128,128]{2,1,0:T(8,128)(2,1)S(1)}, u32[]{:S(2)}, u32[]{:S(2)}) %all-to-all-start.3) | async-done | bytes 1048608 | tf_op jit(solution)/shard_map/all_to_all | solution.py:28
  79.0 1.0 copy.33
  80.0 4.5 %fusion.40 = (f32[4,1024]{1,0:T(4,128)S(1)}, f32[4,1024,192]{1,2,0:T(8,128)}) fusion(pred[4,1024,128]{1,2,0:T(32,128)(4,1)} %broadcast_compare_fusion, pred[192]{0:T(512)(128)(4,1)S(1)} %pad.5.clone, bf16[4,1024,128]{2,1,0:T(8,128)(2,1)S(1)} %bitcast.73, bf16[4,64,128]{2,1,0:T(8,128)(2,1)S(1)} %bitcast.90, bf16[4,128,128]{2,1,0:T(8,128)(2,1)S(1)} %get-tuple-element.33), kind=kOutput, calls=%fused_computation.69 | convolution fusion | flops 409731264 | bytes 4931776 | tf_op jit(solution)/shard_map/while/body/eval_jaxpr/sub | solution.py:85
  84.6 2.4 %fusion.8 = bf16[4,1024,192]{1,2,0:T(8,128)(2,1)S(1)} fusion(f32[4,1024,192]{1,2,0:T(8,128)} %get-tuple-element.31, f32[4,1024]{1,0:T(4,128)S(1)} %get-tuple-element.30), kind=kLoop, calls=%fused_computation.17 | loop fusion | flops 1572864 | bytes 4734976 | tf_op jit(solution)/shard_map/while/body/eval_jaxpr/convert_element_type | solution.py:87
  88.2 3.3 %all-to-all-start.7 = ((f32[4,4,16,128]{3,2,0,1:T(8,128)}), f32[4,4,16,128]{3,2,0,1:T(8,128)S(1)}, u32[]{:S(2)}, u32[]{:S(2)}) async-start(f32[4,4,16,128]{3,2,0,1:T(8,128)} %copy.42), calls=%async_computation.7 | async-start | bytes 262144 | tf_op jit(solution)/shard_map/all_to_all | solution.py:123
  91.6 2.5 %multiply_reduce_fusion = f32[4,1024]{1,0:T(4,128)S(1)} fusion(bf16[4,1024,128]{2,1,0:T(8,128)(2,1)} %bitcast.75, bf16[4,1024,192]{1,2,0:T(8,128)(2,1)S(1)} %fusion.8, bf16[4,64,128]{2,1,0:T(8,128)(2,1)S(1)} %bitcast.92, bf16[4,128,128]{2,1,0:T(8,128)(2,1)S(1)} %copy-done.6), kind=kOutput, calls=%fused_computation.12 | convolution fusion | flops 203288576 | bytes 2834432 | tf_op jit(solution)/shard_map/while/body/eval_jaxpr/irk,ikd->ird/dot_general | solution.py:88
  94.1 2.5 %fusion.1 = bf16[4,1024,192]{1,2,0:T(8,128)(2,1)S(1)} fusion(bf16[4,1024,128]{2,1,0:T(8,128)(2,1)S(1)} %bitcast.77, f32[4,1024]{1,0:T(4,128)S(1)} %multiply_reduce_fusion, f32[4,1024,192]{1,2,0:T(8,128)} %get-tuple-element.31, f32[4,1024]{1,0:T(4,128)S(1)} %get-tuple-element.30, bf16[4,64,128]{2,1,0:T(8,128)(2,1)S(1)} %bitcast.93, ...), kind=kOutput, calls=%fused_computation.4 | convolution fusion | flops 204865536 | bytes 5996544 | tf_op jit(solution)/shard_map/while/body/eval_jaxpr/ird,ikd->irk/dot_general | solution.py:92
  97.9 3.3 %all-to-all-start.5 = ((f32[4,4,16,128]{3,2,0,1:T(8,128)}), f32[4,4,16,128]{3,2,0,1:T(8,128)S(1)}, u32[]{:S(2)}, u32[]{:S(2)}) async-start(f32[4,4,16,128]{3,2,0,1:T(8,128)} %copy.37), calls=%async_computation.5 | async-start | bytes 262144 | tf_op jit(solution)/shard_map/all_to_all | solution.py:122
  102.5 3.3 %all-to-all-done.5 = f32[4,4,16,128]{3,2,0,1:T(8,128)S(1)} async-done(((f32[4,4,16,128]{3,2,0,1:T(8,128)}), f32[4,4,16,128]{3,2,0,1:T(8,128)S(1)}, u32[]{:S(2)}, u32[]{:S(2)}) %all-to-all-start.5) | async-done | bytes 131104 | tf_op jit(solution)/shard_map/all_to_all | solution.py:122
  105.8 3.4 %all-to-all-start.8 = ((bf16[4,128,128]{2,0,1:T(4,128)(2,1)}), bf16[4,128,128]{2,0,1:T(4,128)(2,1)S(1)}, u32[]{:S(2)}, u32[]{:S(2)}) async-start(bf16[4,128,128]{2,0,1:T(4,128)(2,1)} %copy.45), calls=%async_computation.8 | async-start | bytes 262144 | tf_op jit(solution)/shard_map/all_to_all | solution.py:137
  110.5 6.1 %all-to-all-done.8 = bf16[4,128,128]{2,0,1:T(4,128)(2,1)S(1)} async-done(((bf16[4,128,128]{2,0,1:T(4,128)(2,1)}), bf16[4,128,128]{2,0,1:T(4,128)(2,1)S(1)}, u32[]{:S(2)}, u32[]{:S(2)}) %all-to-all-start.8) | async-done | bytes 131104 | tf_op jit(solution)/shard_map/all_to_all | solution.py:137
  116.6 3.4 %all-to-all-start.6 = ((bf16[4,128,128]{2,0,1:T(4,128)(2,1)}), bf16[4,128,128]{2,0,1:T(4,128)(2,1)S(1)}, u32[]{:S(2)}, u32[]{:S(2)}) async-start(bf16[4,128,128]{2,0,1:T(4,128)(2,1)} %copy.40), calls=%async_computation.6 | async-start | bytes 262144 | tf_op jit(solution)/shard_map/all_to_all | solution.py:136
  120.0 1.0 multiply_convert_fusion
  120.9 1.8 %copy.35 = bf16[4,1024,128]{2,0,1:T(4,128)(2,1)} copy(bf16[4,1024,128]{2,1,0:T(8,128)(2,1)S(1)} %multiply_convert_fusion) | data formatting | bytes 2097152 | tf_op jit(solution)/shard_map/while/body/eval_jaxpr/convert_element_type | solution.py:99
  122.7 4.5 %all-to-all-done.6 = bf16[4,128,128]{2,0,1:T(4,128)(2,1)S(1)} async-done(((bf16[4,128,128]{2,0,1:T(4,128)(2,1)}), bf16[4,128,128]{2,0,1:T(4,128)(2,1)S(1)}, u32[]{:S(2)}, u32[]{:S(2)}) %all-to-all-start.6) | async-done | bytes 131104 | tf_op jit(solution)/shard_map/all_to_all | solution.py:136
  127.2 3.6 %all-to-all-start.4 = ((bf16[4,1024,128]{2,0,1:T(4,128)(2,1)}), bf16[4,1024,128]{2,0,1:T(4,128)(2,1)S(1)}, u32[]{:S(2)}, u32[]{:S(2)}) async-start(bf16[4,1024,128]{2,0,1:T(4,128)(2,1)} %copy.35), calls=%async_computation.4 | async-start | bytes 2097152 | tf_op jit(solution)/shard_map/all_to_all | solution.py:135
  132.3 21.9 %all-to-all-done.4 = bf16[4,1024,128]{2,0,1:T(4,128)(2,1)S(1)} async-done(((bf16[4,1024,128]{2,0,1:T(4,128)(2,1)}), bf16[4,1024,128]{2,0,1:T(4,128)(2,1)S(1)}, u32[]{:S(2)}, u32[]{:S(2)}) %all-to-all-start.4) | async-done | bytes 1048608 | tf_op jit(solution)/shard_map/all_to_all | solution.py:135
  154.2 1.2 copy.36
  (55 shorter events, 9.5 us)
Async XLA Ops:
  0.6 0.7 copy-start
  2.5 52.8 %copy-start.5 = (bf16[4,128,128]{2,1,0:T(8,128)(2,1)}, bf16[4,128,128]{2,1,0:T(8,128)(2,1)S(1)}, u32[]{:S(2)}) copy-start(bf16[4,128,128]{2,1,0:T(8,128)(2,1)S(1)} %get-tuple-element.32) | copy-start | bytes 393220
  2.5 77.5 %copy-start.3 = (bf16[4,128,128]{2,1,0:T(8,128)(2,1)}, bf16[4,128,128]{2,1,0:T(8,128)(2,1)S(1)}, u32[]{:S(2)}) copy-start(bf16[4,128,128]{2,1,0:T(8,128)(2,1)S(1)} %get-tuple-element.33) | copy-start | bytes 393220
  49.8 29.2 %all-to-all-start.3 = ((bf16[32,128,128]{2,1,0:T(8,128)(2,1)}), bf16[32,128,128]{2,1,0:T(8,128)(2,1)S(1)}, u32[]{:S(2)}, u32[]{:S(2)}) async-start(bf16[32,128,128]{2,1,0:T(8,128)(2,1)} %param.8), calls=%async_computation.3 | async-start | bytes 2097152 | tf_op jit(solution)/shard_map/all_to_all | solution.py:28
  54.6 29.9 %copy-start.7 = (bf16[4,4,16,128]{3,2,1,0:T(8,128)(2,1)}, bf16[4,4,16,128]{3,2,1,0:T(8,128)(2,1)S(1)}, u32[]{:S(2)}) copy-start(bf16[4,4,16,128]{3,2,1,0:T(8,128)(2,1)S(1)} %copy.30) | copy-start | bytes 196612
  84.5 2.5 %copy-start.1 = (bf16[8,4,128,128]{3,2,0,1:T(8,128)(2,1)S(1)}, bf16[8,4,128,128]{3,2,0,1:T(8,128)(2,1)}, u32[]{:S(2)}) copy-start(bf16[8,4,128,128]{3,2,0,1:T(8,128)(2,1)} %copy.33) | copy-start | bytes 3145732
  84.5 7.1 %copy-start.6 = (bf16[4,128,128]{2,1,0:T(8,128)(2,1)S(1)}, bf16[4,128,128]{2,1,0:T(8,128)(2,1)}, u32[]{:S(2)}) copy-start(bf16[4,128,128]{2,1,0:T(8,128)(2,1)} %copy-done.5) | copy-start | bytes 393220
  84.5 7.1 %copy-start.9 = (bf16[4,4,16,128]{3,2,1,0:T(8,128)(2,1)S(1)}, bf16[4,4,16,128]{3,2,1,0:T(8,128)(2,1)}, u32[]{:S(2)}) copy-start(bf16[4,4,16,128]{3,2,1,0:T(8,128)(2,1)} %copy.32) | copy-start | bytes 196612
  88.2 9.6 %all-to-all-start.7 = ((f32[4,4,16,128]{3,2,0,1:T(8,128)}), f32[4,4,16,128]{3,2,0,1:T(8,128)S(1)}, u32[]{:S(2)}, u32[]{:S(2)}) async-start(f32[4,4,16,128]{3,2,0,1:T(8,128)} %copy.42), calls=%async_computation.7 | async-start | bytes 262144 | tf_op jit(solution)/shard_map/all_to_all | solution.py:123
  91.6 2.5 %copy-start.2 = (bf16[8,4,128,128]{3,2,0,1:T(8,128)(2,1)S(1)}, bf16[8,4,128,128]{3,2,0,1:T(8,128)(2,1)}, u32[]{:S(2)}) copy-start(bf16[8,4,128,128]{3,2,0,1:T(8,128)(2,1)} %copy.33) | copy-start | bytes 3145732
  97.2 22.8 %copy-start.4 = (bf16[4,128,128]{2,1,0:T(8,128)(2,1)S(1)}, bf16[4,128,128]{2,1,0:T(8,128)(2,1)}, u32[]{:S(2)}) copy-start(bf16[4,128,128]{2,1,0:T(8,128)(2,1)} %copy-done.3) | copy-start | bytes 393220
  97.2 22.8 %copy-start.8 = (bf16[4,4,16,128]{3,2,1,0:T(8,128)(2,1)S(1)}, bf16[4,4,16,128]{3,2,1,0:T(8,128)(2,1)}, u32[]{:S(2)}) copy-start(bf16[4,4,16,128]{3,2,1,0:T(8,128)(2,1)} %copy-done.7) | copy-start | bytes 196612
  97.9 7.9 %all-to-all-start.5 = ((f32[4,4,16,128]{3,2,0,1:T(8,128)}), f32[4,4,16,128]{3,2,0,1:T(8,128)S(1)}, u32[]{:S(2)}, u32[]{:S(2)}) async-start(f32[4,4,16,128]{3,2,0,1:T(8,128)} %copy.37), calls=%async_computation.5 | async-start | bytes 262144 | tf_op jit(solution)/shard_map/all_to_all | solution.py:122
  105.8 10.8 %all-to-all-start.8 = ((bf16[4,128,128]{2,0,1:T(4,128)(2,1)}), bf16[4,128,128]{2,0,1:T(4,128)(2,1)S(1)}, u32[]{:S(2)}, u32[]{:S(2)}) async-start(bf16[4,128,128]{2,0,1:T(4,128)(2,1)} %copy.45), calls=%async_computation.8 | async-start | bytes 262144 | tf_op jit(solution)/shard_map/all_to_all | solution.py:137
  116.6 10.7 %all-to-all-start.6 = ((bf16[4,128,128]{2,0,1:T(4,128)(2,1)}), bf16[4,128,128]{2,0,1:T(4,128)(2,1)S(1)}, u32[]{:S(2)}, u32[]{:S(2)}) async-start(bf16[4,128,128]{2,0,1:T(4,128)(2,1)} %copy.40), calls=%async_computation.6 | async-start | bytes 262144 | tf_op jit(solution)/shard_map/all_to_all | solution.py:136
  127.2 26.9 %all-to-all-start.4 = ((bf16[4,1024,128]{2,0,1:T(4,128)(2,1)}), bf16[4,1024,128]{2,0,1:T(4,128)(2,1)S(1)}, u32[]{:S(2)}, u32[]{:S(2)}) async-start(bf16[4,1024,128]{2,0,1:T(4,128)(2,1)} %copy.35), calls=%async_computation.4 | async-start | bytes 2097152 | tf_op jit(solution)/shard_map/all_to_all | solution.py:135
where the time goes:
time: 156 us; the launch traced here: 155 us
  waiting for transfers between devices  59.4 us (38%)
  blocking collectives  46 us (29%)
  starting transfers between devices  20.6 us (13%)
  local copies, waits for them, and re-layouts  12.4 us (8%)
  matrix products  12.4 us (8%)
  other arithmetic  3.66 us (2%)
    all_to_all x1, blocking collectives, body(): lax.all_to_all(packed_query, 'ulysses', split_axis=0, concat_axis=1, tile...  31.4 us
    all_to_all x1, waiting for transfers between devices, body(): lax.all_to_all(packed_grad, 'ulysses', split_axis=0, concat_axis=1, tiled...  23.6 us
    all_to_all x1, waiting for transfers between devices, body(): lax.all_to_all(query_out, 'ulysses', split_axis=1, concat_axis=0, tiled=T...  21.9 us
    all_to_all x1, blocking collectives, body(): lax.all_to_all(jnp.take(block_keys, requested, axis=1), 'blk', split_axis...  8.16 us
    all_to_all x1, blocking collectives, body(): lax.all_to_all(jnp.take(block_values, requested, axis=1), 'blk', split_ax...  6.47 us
    all_to_all x1, waiting for transfers between devices, body(): lax.all_to_all(value_share, 'ulysses', split_axis=1, concat_axis=0, tiled...  6.08 us
    all_to_all x1, waiting for transfers between devices, body(): lax.all_to_all(key_share, 'ulysses', split_axis=1, concat_axis=0, tiled=T...  4.52 us
    sub x1, matrix products, attend(): expsum = jnp.where(visible, jnp.exp(scores - row_max), 0.0)  4.49 us
  transfers between devices with their start and end apart: 6, of which 5 were waited for; matrix products, arithmetic and copies ran while one was open for 10% of the time, Pallas kernels for 0%

commit v1 on v0

--- a/solution.py
+++ b/solution.py
@@ -5,6 +5,30 @@
 from jax.sharding import PartitionSpec as P
 
 KB = 16
+
+
+def split_up(value, dim, size):
+    dims = value.shape
+    blocks = value.reshape(*dims[:dim], size, dims[dim] // size, *dims[dim + 1 :])
+    return jnp.moveaxis(blocks, dim, 0)
+
+
+def in_order(blocks, dim):
+    blocks = jnp.moveaxis(blocks, 0, dim)
+    shape = blocks.shape
+    return blocks.reshape(*shape[:dim], shape[dim] * shape[dim + 1], *shape[dim + 2 :])
+
+
+def rotated_exchange(x, axis, split_dim, concat_dim):
+    size, index = (lax.axis_size(axis), lax.axis_index(axis))
+    blocks = split_up(x, split_dim, size)
+    filled = blocks
+    for step in range(1, size):
+        target, source = ((index + step) % size, (index - step) % size)
+        sent = lax.dynamic_index_in_dim(blocks, target, 0)
+        partner_block = lax.ppermute(sent, axis, [(i, (i + step) % size) for i in range(size)])
+        filled = lax.dynamic_update_slice_in_dim(filled, partner_block, source, axis=0)
+    return in_order(filled, concat_dim)
 
 
 def body(query_rows, out_grad, key_rows, value_rows, routes):
@@ -25,7 +49,7 @@
     packed_grad = out_grad.reshape(head_count * sub_count, sub_length, head_dim)
     local_query, local_grad = (
         lax.all_to_all(packed_query, "ulysses", split_axis=0, concat_axis=1, tiled=True),
-        lax.all_to_all(packed_grad, "ulysses", split_axis=0, concat_axis=1, tiled=True),
+        rotated_exchange(packed_grad, "ulysses", 0, 1),
     )
     first_head = my_rank * item_count // sub_count
     own_keys = lax.dynamic_slice_in_dim(key_rows, first_head, item_count, 0)

time: 156 us -> 204 us (1.31)
  local copies, waits for them, and re-layouts: 12.4 us -> 59.5 us
  blocking collectives: 46 us -> 14.6 us
  starting transfers between devices: 20.6 us -> 42.1 us
  waiting for transfers between devices: 59.4 us -> 75.1 us
  matrix products: 12.4 us -> 7.34 us
    dynamic_update_slice x0 -> x7, local copies, waits for them, and re-layouts: none -> 41.8 us  [rotated_exchange(): lax.dynamic_update_slice_in_dim(filled, partner_block, source, axis=0)]
    ppermute x0 -> x7, waiting for transfers between devices: none -> 35.9 us  [rotated_exchange(): lax.ppermute(sent, axis, [(i, (i + step) % size) for i in range(size)])]
    all_to_all x1 -> x0, blocking collectives: 31.4 us -> none  [body(): lax.all_to_all(packed_query, 'ulysses', split_axis=0, concat_axis=1, tile...]
    all_to_all x1, waiting for transfers between devices: 23.6 us -> 0.01 us  [body(): lax.all_to_all(packed_query, 'ulysses', split_axis=0, concat_axis=1, tile...]
    ppermute x0 -> x7, starting transfers between devices: none -> 19.3 us  [rotated_exchange(): lax.ppermute(sent, axis, [(i, (i + step) % size) for i in range(size)])]
    all_to_all x1, waiting for transfers between devices: 0.01 us -> 3.3 us  [body(): lax.all_to_all(far_value_grad, 'blk', split_axis=1, concat_axis=1, tiled=...]
    dynamic_slice x0 -> x1, local copies, waits for them, and re-layouts: none -> 2.78 us  [rotated_exchange(): sent = lax.dynamic_index_in_dim(blocks, target, 0)]
    all_to_all x1, starting transfers between devices: 3.59 us -> 5.83 us  [body(): lax.all_to_all(packed_query, 'ulysses', split_axis=0, concat_axis=1, tile...]
  transfers between devices with their start and end apart: 6 -> 13, of which waited for: 5 -> 7; matrix products, arithmetic and copies ran while one was open for 10% -> 27% of each run, Pallas kernels for 0% -> 0%
where the time goes in v1:
time: 204 us; the launch traced here: 203 us
  waiting for transfers between devices  75.1 us (37%)
  local copies, waits for them, and re-layouts  59.5 us (29%)
  starting transfers between devices  42.1 us (21%)
  blocking collectives  14.6 us (7%)
  matrix products  7.34 us (4%)
  other arithmetic  2.89 us (1%)
    dynamic_update_slice x7, local copies, waits for them, and re-layouts, rotated_exchange(): lax.dynamic_update_slice_in_dim(filled, partner_block, source, axis=0)  41.8 us
    ppermute x7, waiting for transfers between devices, rotated_exchange(): lax.ppermute(sent, axis, [(i, (i + step) % size) for i in range(size)])  35.9 us
    all_to_all x1, waiting for transfers between devices, body(): lax.all_to_all(query_out, 'ulysses', split_axis=1, concat_axis=0, tiled=T...  22.1 us
    ppermute x7, starting transfers between devices, rotated_exchange(): lax.ppermute(sent, axis, [(i, (i + step) % size) for i in range(size)])  19.3 us
    all_to_all x1, blocking collectives, body(): lax.all_to_all(jnp.take(block_values, requested, axis=1), 'blk', split_ax...  8.16 us
    all_to_all x1, blocking collectives, body(): lax.all_to_all(jnp.take(block_keys, requested, axis=1), 'blk', split_axis...  6.47 us
    all_to_all x1, waiting for transfers between devices, body(): lax.all_to_all(key_share, 'ulysses', split_axis=1, concat_axis=0, tiled=T...  6.02 us
    all_to_all x1, starting transfers between devices, body(): lax.all_to_all(packed_query, 'ulysses', split_axis=0, concat_axis=1, tile...  5.83 us
  transfers between devices with their start and end apart: 13, of which 7 were waited for; matrix products, arithmetic and copies ran while one was open for 27% of the time, Pallas kernels for 0%

profile of v1, /device:TPU:0, one launch (start us, length us, event | category | flops | bytes accessed | tf_op | source)
XLA Modules:
  0.0 202.7 jit_solution(9597339206591309734)
XLA Ops:
  3.8 8.2 %all_to_all.74 = bf16[4,4,16,128]{3,2,0,1:T(8,128)(2,1)S(1)} all-to-all(bf16[4,4,16,128]{3,2,0,1:T(8,128)(2,1)S(1)} %get-tuple-element.35), channel_id=1, replica_groups=mesh['blk'=4,'ulysses'=8] {'blk'}, dimensions={1} | all-to-all | bytes 131072 | tf_op jit(solution)/shard_map/all_to_all | solution.py:65
  11.9 6.5 %all_to_all.75 = bf16[4,4,16,128]{3,2,0,1:T(8,128)(2,1)S(1)} all-to-all(bf16[4,4,16,128]{3,2,0,1:T(8,128)(2,1)S(1)} %get-tuple-element.48), channel_id=1, replica_groups=mesh['blk'=4,'ulysses'=8] {'blk'}, dimensions={1} | all-to-all | bytes 131072 | tf_op jit(solution)/shard_map/all_to_all | solution.py:62
  18.4 5.8 %all-to-all-start.1 = ((bf16[32,128,128]{2,1,0:T(8,128)(2,1)}), bf16[32,128,128]{2,1,0:T(8,128)(2,1)}, u32[]{:S(2)}, u32[]{:S(2)}) async-start(bf16[32,128,128]{2,1,0:T(8,128)(2,1)} %param.7), calls=%async_computation.1 | async-start | bytes 2097152 | tf_op jit(solution)/shard_map/all_to_all | solution.py:51
  27.8 4.7 %collective-permute-start.6 = (bf16[1,4,128,128]{2,0,3,1:T(2,128)(2,1)}, bf16[1,4,128,128]{2,0,3,1:T(2,128)(2,1)S(1)}, u32[]{:S(2)}, u32[]{:S(2)}) collective-permute-start(bf16[1,4,128,128]{2,0,3,1:T(2,128)(2,1)} %get-tuple-element.28), channel_id=1, source_target_pairs={{0,7},{1,0},{2,1},{3,2},{4,3},{5,4},{6,5},{7,6},{8,15},{9,8},{10,9... | collective-permute-start | bytes 393224 | tf_op jit(solution)/shard_map/ppermute | solution.py:29
  36.7 30.9 %collective-permute-done.1 = bf16[1,4,128,128]{2,0,3,1:T(2,128)(2,1)S(1)} collective-permute-done((bf16[1,4,128,128]{2,0,3,1:T(2,128)(2,1)S(1)}, bf16[1,4,128,128]{2,0,3,1:T(2,128)(2,1)S(1)}, u32[]{:S(2)}, u32[]{:S(2)}) %collective-permute-start.1) | collective-permute-done | bytes 131104 | tf_op jit(solution)/shard_map/ppermute | solution.py:29
  67.7 10.5 %collective-permute-start.3 = (bf16[1,4,128,128]{2,0,3,1:T(2,128)(2,1)}, bf16[1,4,128,128]{2,0,3,1:T(2,128)(2,1)S(1)}, u32[]{:S(2)}, u32[]{:S(2)}) collective-permute-start(bf16[1,4,128,128]{2,0,3,1:T(2,128)(2,1)} %get-tuple-element.31), channel_id=1, source_target_pairs={{0,4},{1,5},{2,6},{3,7},{4,0},{5,1},{6,2},{7,3},{8,12},{9,13},{10,... | collective-permute-start | bytes 393224 | tf_op jit(solution)/shard_map/ppermute | solution.py:29
  79.0 5.9 %dynamic_update_slice.23 = bf16[8,4,128,128]{2,0,3,1:T(8,128)(2,1)S(1)} dynamic-update-slice(bf16[8,4,128,128]{2,0,3,1:T(8,128)(2,1)S(1)} %copy.49, bf16[1,4,128,128]{2,0,3,1:T(2,128)(2,1)S(1)} %collective-permute-done, s32[]{:T(128)S(6)} %select_n.170, s32[]{:T(128)} %constant.187.clone.1, s32[]{:T(128)} %constant.187.clone.1, s32[]{:T(128)} %constant.187.clone.1) | dynamic-update-slice | bytes 262148 | tf_op jit(solution)/shard_map/dynamic_update_slice | solution.py:30
  84.9 5.9 %dynamic_update_slice.24 = bf16[8,4,128,128]{2,0,3,1:T(8,128)(2,1)S(1)} dynamic-update-slice(bf16[8,4,128,128]{2,0,3,1:T(8,128)(2,1)S(1)} %dynamic_update_slice.23, bf16[1,4,128,128]{2,0,3,1:T(2,128)(2,1)S(1)} %collective-permute-done.1, s32[]{:T(128)S(6)} %select_n.174, s32[]{:T(128)} %constant.187.clone.1, s32[]{:T(128)} %constant.187.clone.1, s32[]{:T(128)} %constant.187.clone.1) | dynamic-update-slice | bytes 262148 | tf_op jit(solution)/shard_map/dynamic_update_slice | solution.py:30
  90.8 4.9 %collective-permute-done.2 = bf16[1,4,128,128]{2,0,3,1:T(2,128)(2,1)} collective-permute-done((bf16[1,4,128,128]{2,0,3,1:T(2,128)(2,1)}, bf16[1,4,128,128]{2,0,3,1:T(2,128)(2,1)}, u32[]{:S(2)}, u32[]{:S(2)}) %collective-permute-start.2) | collective-permute-done | bytes 131104 | tf_op jit(solution)/shard_map/ppermute | solution.py:29
  95.7 6.6 %dynamic_update_slice.25 = bf16[8,4,128,128]{2,0,3,1:T(8,128)(2,1)S(1)} dynamic-update-slice(bf16[8,4,128,128]{2,0,3,1:T(8,128)(2,1)S(1)} %dynamic_update_slice.24, bf16[1,4,128,128]{2,0,3,1:T(2,128)(2,1)} %collective-permute-done.2, s32[]{:T(128)S(6)} %select_n.178, s32[]{:T(128)} %constant.187.clone.1, s32[]{:T(128)} %constant.187.clone.1, s32[]{:T(128)} %constant.187.clone.1) | dynamic-update-slice | bytes 262148 | tf_op jit(solution)/shard_map/dynamic_update_slice | solution.py:30
  102.3 5.9 %dynamic_update_slice.26 = bf16[8,4,128,128]{2,0,3,1:T(8,128)(2,1)S(1)} dynamic-update-slice(bf16[8,4,128,128]{2,0,3,1:T(8,128)(2,1)S(1)} %dynamic_update_slice.25, bf16[1,4,128,128]{2,0,3,1:T(2,128)(2,1)S(1)} %collective-permute-done.3, s32[]{:T(128)S(6)} %select_n.182, s32[]{:T(128)} %constant.187.clone.1, s32[]{:T(128)} %constant.187.clone.1, s32[]{:T(128)} %constant.187.clone.1) | dynamic-update-slice | bytes 262148 | tf_op jit(solution)/shard_map/dynamic_update_slice | solution.py:30
  108.2 5.9 %dynamic_update_slice.27 = bf16[8,4,128,128]{2,0,3,1:T(8,128)(2,1)S(1)} dynamic-update-slice(bf16[8,4,128,128]{2,0,3,1:T(8,128)(2,1)S(1)} %dynamic_update_slice.26, bf16[1,4,128,128]{2,0,3,1:T(2,128)(2,1)S(1)} %collective-permute-done.4, s32[]{:T(128)S(6)} %select_n.186, s32[]{:T(128)} %constant.187.clone.1, s32[]{:T(128)} %constant.187.clone.1, s32[]{:T(128)} %constant.187.clone.1) | dynamic-update-slice | bytes 262148 | tf_op jit(solution)/shard_map/dynamic_update_slice | solution.py:30
  114.1 5.9 %dynamic_update_slice.28 = bf16[8,4,128,128]{2,0,3,1:T(8,128)(2,1)S(1)} dynamic-update-slice(bf16[8,4,128,128]{2,0,3,1:T(8,128)(2,1)S(1)} %dynamic_update_slice.27, bf16[1,4,128,128]{2,0,3,1:T(2,128)(2,1)S(1)} %collective-permute-done.5, s32[]{:T(128)S(6)} %select_n.190, s32[]{:T(128)} %constant.187.clone.1, s32[]{:T(128)} %constant.187.clone.1, s32[]{:T(128)} %constant.187.clone.1) | dynamic-update-slice | bytes 262148 | tf_op jit(solution)/shard_map/dynamic_update_slice | solution.py:30
  120.0 5.9 %dynamic_update_slice.29 = bf16[8,4,128,128]{2,0,3,1:T(8,128)(2,1)S(1)} dynamic-update-slice(bf16[8,4,128,128]{2,0,3,1:T(8,128)(2,1)S(1)} %dynamic_update_slice.28, bf16[1,4,128,128]{2,0,3,1:T(2,128)(2,1)S(1)} %collective-permute-done.6, s32[]{:T(128)S(6)} %select_n.194, s32[]{:T(128)} %constant.187.clone.1, s32[]{:T(128)} %constant.187.clone.1, s32[]{:T(128)} %constant.187.clone.1) | dynamic-update-slice | bytes 262148 | tf_op jit(solution)/shard_map/dynamic_update_slice | solution.py:30
  127.7 3.3 %fusion.41 = (f32[4,1024]{1,0:T(4,128)S(1)}, f32[4,1024,192]{1,2,0:T(8,128)}) fusion(pred[4,1024,128]{1,2,0:T(32,128)(4,1)S(1)} %broadcast_compare_fusion, pred[192]{0:T(512)(128)(4,1)S(1)} %pad.5.clone, bf16[4,1024,128]{2,1,0:T(8,128)(2,1)S(1)} %bitcast.72, bf16[4,64,128]{2,1,0:T(8,128)(2,1)S(1)} %bitcast.85, bf16[4,128,128]{2,1,0:T(8,128)(2,1)S(1)} %get-tuple-element.52), kind=kOutput, calls=%fused_computation.77 | convolution fusion | flops 409731264 | bytes 4931776 | tf_op jit(solution)/shard_map/while/body/eval_jaxpr/sub | solution.py:109
  137.2 3.3 %all-to-all-start.4 = ((f32[4,4,16,128]{3,2,0,1:T(8,128)}), f32[4,4,16,128]{3,2,0,1:T(8,128)S(1)}, u32[]{:S(2)}, u32[]{:S(2)}) async-start(f32[4,4,16,128]{3,2,0,1:T(8,128)} %copy.60), calls=%async_computation.4 | async-start | bytes 262144 | tf_op jit(solution)/shard_map/all_to_all | solution.py:146
  145.1 3.3 %all-to-all-start.6 = ((f32[4,4,16,128]{3,2,0,1:T(8,128)}), f32[4,4,16,128]{3,2,0,1:T(8,128)S(1)}, u32[]{:S(2)}, u32[]{:S(2)}) async-start(f32[4,4,16,128]{3,2,0,1:T(8,128)} %copy.66), calls=%async_computation.6 | async-start | bytes 262144 | tf_op jit(solution)/shard_map/all_to_all | solution.py:147
  149.7 3.3 %all-to-all-done.6 = f32[4,4,16,128]{3,2,0,1:T(8,128)S(1)} async-done(((f32[4,4,16,128]{3,2,0,1:T(8,128)}), f32[4,4,16,128]{3,2,0,1:T(8,128)S(1)}, u32[]{:S(2)}, u32[]{:S(2)}) %all-to-all-start.6) | async-done | bytes 131104 | tf_op jit(solution)/shard_map/all_to_all | solution.py:147
  153.0 3.4 %all-to-all-start.5 = ((bf16[4,128,128]{2,0,1:T(4,128)(2,1)}), bf16[4,128,128]{2,0,1:T(4,128)(2,1)S(1)}, u32[]{:S(2)}, u32[]{:S(2)}) async-start(bf16[4,128,128]{2,0,1:T(4,128)(2,1)} %copy.63), calls=%async_computation.5 | async-start | bytes 262144 | tf_op jit(solution)/shard_map/all_to_all | solution.py:160
  157.6 6.0 %all-to-all-done.5 = bf16[4,128,128]{2,0,1:T(4,128)(2,1)S(1)} async-done(((bf16[4,128,128]{2,0,1:T(4,128)(2,1)}), bf16[4,128,128]{2,0,1:T(4,128)(2,1)S(1)}, u32[]{:S(2)}, u32[]{:S(2)}) %all-to-all-start.5) | async-done | bytes 131104 | tf_op jit(solution)/shard_map/all_to_all | solution.py:160
  163.6 3.4 %all-to-all-start.7 = ((bf16[4,128,128]{2,0,1:T(4,128)(2,1)}), bf16[4,128,128]{2,0,1:T(4,128)(2,1)S(1)}, u32[]{:S(2)}, u32[]{:S(2)}) async-start(bf16[4,128,128]{2,0,1:T(4,128)(2,1)} %copy.69), calls=%async_computation.7 | async-start | bytes 262144 | tf_op jit(solution)/shard_map/all_to_all | solution.py:161
  169.8 4.5 %all-to-all-done.7 = bf16[4,128,128]{2,0,1:T(4,128)(2,1)S(1)} async-done(((bf16[4,128,128]{2,0,1:T(4,128)(2,1)}), bf16[4,128,128]{2,0,1:T(4,128)(2,1)S(1)}, u32[]{:S(2)}, u32[]{:S(2)}) %all-to-all-start.7) | async-done | bytes 131104 | tf_op jit(solution)/shard_map/all_to_all | solution.py:161
  174.3 3.6 %all-to-all-start.3 = ((bf16[4,1024,128]{2,0,1:T(4,128)(2,1)}), bf16[4,1024,128]{2,0,1:T(4,128)(2,1)S(1)}, u32[]{:S(2)}, u32[]{:S(2)}) async-start(bf16[4,1024,128]{2,0,1:T(4,128)(2,1)} %copy.58), calls=%async_computation.3 | async-start | bytes 2097152 | tf_op jit(solution)/shard_map/all_to_all | solution.py:159
  179.3 22.1 %all-to-all-done.3 = bf16[4,1024,128]{2,0,1:T(4,128)(2,1)S(1)} async-done(((bf16[4,1024,128]{2,0,1:T(4,128)(2,1)}), bf16[4,1024,128]{2,0,1:T(4,128)(2,1)S(1)}, u32[]{:S(2)}, u32[]{:S(2)}) %all-to-all-start.3) | async-done | bytes 1048608 | tf_op jit(solution)/shard_map/all_to_all | solution.py:159
  (81 shorter events, 32.0 us)
Async XLA Ops:
  0.6 23.6 %copy-start.6 = (bf16[32,128,128]{2,1,0:T(8,128)(2,1)S(1)}, bf16[32,128,128]{2,1,0:T(8,128)(2,1)}, u32[]{:S(2)}) copy-start(bf16[32,128,128]{2,1,0:T(8,128)(2,1)} %param.8) | copy-start | bytes 3145732
  2.5 125.2 %copy-start.7 = (bf16[4,128,128]{2,1,0:T(8,128)(2,1)}, bf16[4,128,128]{2,1,0:T(8,128)(2,1)S(1)}, u32[]{:S(2)}) copy-start(bf16[4,128,128]{2,1,0:T(8,128)(2,1)S(1)} %get-tuple-element.52) | copy-start | bytes 393220
  18.4 108.0 %all-to-all-start.1 = ((bf16[32,128,128]{2,1,0:T(8,128)(2,1)}), bf16[32,128,128]{2,1,0:T(8,128)(2,1)}, u32[]{:S(2)}, u32[]{:S(2)}) async-start(bf16[32,128,128]{2,1,0:T(8,128)(2,1)} %param.7), calls=%async_computation.1 | async-start | bytes 2097152 | tf_op jit(solution)/shard_map/all_to_all | solution.py:51
  27.8 92.2 %collective-permute-start.6 = (bf16[1,4,128,128]{2,0,3,1:T(2,128)(2,1)}, bf16[1,4,128,128]{2,0,3,1:T(2,128)(2,1)S(1)}, u32[]{:S(2)}, u32[]{:S(2)}) collective-permute-start(bf16[1,4,128,128]{2,0,3,1:T(2,128)(2,1)} %get-tuple-element.28), channel_id=1, source_target_pairs={{0,7},{1,0},{2,1},{3,2},{4,3},{5,4},{6,5},{7,6},{8,15},{9,8},{10,9... | collective-permute-start | bytes 393224 | tf_op jit(solution)/shard_map/ppermute | solution.py:29
  32.5 81.6 %collective-permute-start.5 = (bf16[1,4,128,128]{2,0,3,1:T(2,128)(2,1)}, bf16[1,4,128,128]{2,0,3,1:T(2,128)(2,1)S(1)}, u32[]{:S(2)}, u32[]{:S(2)}) collective-permute-start(bf16[1,4,128,128]{2,0,3,1:T(2,128)(2,1)} %get-tuple-element.29), channel_id=1, source_target_pairs={{0,6},{1,7},{2,0},{3,1},{4,2},{5,3},{6,4},{7,5},{8,14},{9,15},{10,... | collective-permute-start | bytes 393224 | tf_op jit(solution)/shard_map/ppermute | solution.py:29
  33.1 75.1 %collective-permute-start.4 = (bf16[1,4,128,128]{2,0,3,1:T(2,128)(2,1)}, bf16[1,4,128,128]{2,0,3,1:T(2,128)(2,1)S(1)}, u32[]{:S(2)}, u32[]{:S(2)}) collective-permute-start(bf16[1,4,128,128]{2,0,3,1:T(2,128)(2,1)} %get-tuple-element.30), channel_id=1, source_target_pairs={{0,5},{1,6},{2,7},{3,0},{4,1},{5,2},{6,3},{7,4},{8,13},{9,14},{10,... | collective-permute-start | bytes 393224 | tf_op jit(solution)/shard_map/ppermute | solution.py:29
  33.1 34.6 %collective-permute-start.1 = (bf16[1,4,128,128]{2,0,3,1:T(2,128)(2,1)S(1)}, bf16[1,4,128,128]{2,0,3,1:T(2,128)(2,1)S(1)}, u32[]{:S(2)}, u32[]{:S(2)}) collective-permute-start(bf16[1,4,128,128]{2,0,3,1:T(2,128)(2,1)S(1)} %get-tuple-element.33), channel_id=1, source_target_pairs={{0,2},{1,3},{2,4},{3,5},{4,6},{5,7},{6,0},{7,1},{8,10},{9,11},{10,... | collective-permute-start | bytes 393224 | tf_op jit(solution)/shard_map/ppermute | solution.py:29
  34.5 43.7 %collective-permute-start = (bf16[1,4,128,128]{2,0,3,1:T(2,128)(2,1)S(1)}, bf16[1,4,128,128]{2,0,3,1:T(2,128)(2,1)S(1)}, u32[]{:S(2)}, u32[]{:S(2)}) collective-permute-start(bf16[1,4,128,128]{2,0,3,1:T(2,128)(2,1)S(1)} %get-tuple-element.34), channel_id=1, source_target_pairs={{0,1},{1,2},{2,3},{3,4},{4,5},{5,6},{6,7},{7,0},{8,9},{9,10},{10,1... | collective-permute-start | bytes 393224 | tf_op jit(solution)/shard_map/ppermute | solution.py:29
  67.7 34.6 %collective-permute-start.3 = (bf16[1,4,128,128]{2,0,3,1:T(2,128)(2,1)}, bf16[1,4,128,128]{2,0,3,1:T(2,128)(2,1)S(1)}, u32[]{:S(2)}, u32[]{:S(2)}) collective-permute-start(bf16[1,4,128,128]{2,0,3,1:T(2,128)(2,1)} %get-tuple-element.31), channel_id=1, source_target_pairs={{0,4},{1,5},{2,6},{3,7},{4,0},{5,1},{6,2},{7,3},{8,12},{9,13},{10,... | collective-permute-start | bytes 393224 | tf_op jit(solution)/shard_map/ppermute | solution.py:29
  78.2 17.5 %collective-permute-start.2 = (bf16[1,4,128,128]{2,0,3,1:T(2,128)(2,1)}, bf16[1,4,128,128]{2,0,3,1:T(2,128)(2,1)}, u32[]{:S(2)}, u32[]{:S(2)}) collective-permute-start(bf16[1,4,128,128]{2,0,3,1:T(2,128)(2,1)} %get-tuple-element.32), channel_id=1, source_target_pairs={{0,3},{1,4},{2,5},{3,6},{4,7},{5,0},{6,1},{7,2},{8,11},{9,12},{10,... | collective-permute-start | bytes 393224 | tf_op jit(solution)/shard_map/ppermute | solution.py:29
  79.0 48.7 %copy-start.9 = (bf16[4,4,16,128]{3,2,1,0:T(8,128)(2,1)}, bf16[4,4,16,128]{3,2,1,0:T(8,128)(2,1)S(1)}, u32[]{:S(2)}) copy-start(bf16[4,4,16,128]{3,2,1,0:T(8,128)(2,1)S(1)} %copy.46) | copy-start | bytes 196612
  127.7 3.3 %copy-start.1 = (bf16[8,4,128,128]{3,2,0,1:T(8,128)(2,1)}, bf16[8,4,128,128]{3,2,0,1:T(8,128)(2,1)S(1)}, u32[]{:S(2)}) copy-start(bf16[8,4,128,128]{3,2,0,1:T(8,128)(2,1)S(1)} %copy.47) | copy-start | bytes 3145732
  131.0 2.5 %copy-start.11 = (bf16[4,4,16,128]{3,2,1,0:T(8,128)(2,1)S(1)}, bf16[4,4,16,128]{3,2,1,0:T(8,128)(2,1)}, u32[]{:S(2)}) copy-start(bf16[4,4,16,128]{3,2,1,0:T(8,128)(2,1)} %copy.56) | copy-start | bytes 196612
  131.0 3.1 %copy-start.3 = (f32[4,1024,192]{1,2,0:T(8,128)S(1)}, f32[4,1024,192]{1,2,0:T(8,128)}, u32[]{:S(2)}) copy-start(f32[4,1024,192]{1,2,0:T(8,128)} %get-tuple-element.50) | copy-start | bytes 9437188
  134.1 1.2 copy-start.2
  135.3 1.2 copy-start.4
  137.2 7.9 %all-to-all-start.4 = ((f32[4,4,16,128]{3,2,0,1:T(8,128)}), f32[4,4,16,128]{3,2,0,1:T(8,128)S(1)}, u32[]{:S(2)}, u32[]{:S(2)}) async-start(f32[4,4,16,128]{3,2,0,1:T(8,128)} %copy.60), calls=%async_computation.4 | async-start | bytes 262144 | tf_op jit(solution)/shard_map/all_to_all | solution.py:146
  141.1 25.9 %copy-start.5 = (bf16[4,1024,192]{1,2,0:T(8,128)(2,1)S(1)}, bf16[4,1024,192]{1,2,0:T(8,128)(2,1)}, u32[]{:S(2)}) copy-start(bf16[4,1024,192]{1,2,0:T(8,128)(2,1)} %copy-done.4) | copy-start | bytes 4718596
  141.1 25.9 %copy-start.8 = (bf16[4,128,128]{2,1,0:T(8,128)(2,1)S(1)}, bf16[4,128,128]{2,1,0:T(8,128)(2,1)}, u32[]{:S(2)}) copy-start(bf16[4,128,128]{2,1,0:T(8,128)(2,1)} %copy-done.7) | copy-start | bytes 393220
  141.1 25.9 %copy-start.10 = (bf16[4,4,16,128]{3,2,1,0:T(8,128)(2,1)S(1)}, bf16[4,4,16,128]{3,2,1,0:T(8,128)(2,1)}, u32[]{:S(2)}) copy-start(bf16[4,4,16,128]{3,2,1,0:T(8,128)(2,1)} %copy-done.9) | copy-start | bytes 196612
  145.1 7.9 %all-to-all-start.6 = ((f32[4,4,16,128]{3,2,0,1:T(8,128)}), f32[4,4,16,128]{3,2,0,1:T(8,128)S(1)}, u32[]{:S(2)}, u32[]{:S(2)}) async-start(f32[4,4,16,128]{3,2,0,1:T(8,128)} %copy.66), calls=%async_computation.6 | async-start | bytes 262144 | tf_op jit(solution)/shard_map/all_to_all | solution.py:147
  153.0 10.7 %all-to-all-start.5 = ((bf16[4,128,128]{2,0,1:T(4,128)(2,1)}), bf16[4,128,128]{2,0,1:T(4,128)(2,1)S(1)}, u32[]{:S(2)}, u32[]{:S(2)}) async-start(bf16[4,128,128]{2,0,1:T(4,128)(2,1)} %copy.63), calls=%async_computation.5 | async-start | bytes 262144 | tf_op jit(solution)/shard_map/all_to_all | solution.py:160
  163.6 10.7 %all-to-all-start.7 = ((bf16[4,128,128]{2,0,1:T(4,128)(2,1)}), bf16[4,128,128]{2,0,1:T(4,128)(2,1)S(1)}, u32[]{:S(2)}, u32[]{:S(2)}) async-start(bf16[4,128,128]{2,0,1:T(4,128)(2,1)} %copy.69), calls=%async_computation.7 | async-start | bytes 262144 | tf_op jit(solution)/shard_map/all_to_all | solution.py:161
  174.3 27.2 %all-to-all-start.3 = ((bf16[4,1024,128]{2,0,1:T(4,128)(2,1)}), bf16[4,1024,128]{2,0,1:T(4,128)(2,1)S(1)}, u32[]{:S(2)}, u32[]{:S(2)}) async-start(bf16[4,1024,128]{2,0,1:T(4,128)(2,1)} %copy.58), calls=%async_computation.3 | async-start | bytes 2097152 | tf_op jit(solution)/shard_map/all_to_all | solution.py:159
  (1 other events, 0.7 us)
